TPU v7x, 32 devices: a whole 2x2x4 slice. The times are simulated.
32 devices in a mesh: dp: 16 (over z, y, core), pipe: 2 (over x).
Axes of the slice: x: 2, y: 2, z: 4, core: 2. Of those that a mesh axis runs over, the one named last changes fastest.
Arguments:
- master: float32 [2, 2, 8192, 256], P('pipe', None, 'dp'), may hold values from -12 to 12
- grads: float32 [2, 2, 8192, 256], P('pipe', None, 'dp'), may hold values from -60 to 60
- first_moment: float32 [2, 2, 8192, 256], P('pipe', None, 'dp'), may hold values from -4 to 4
- second_moment: float32 [2, 2, 8192, 256], P('pipe', None, 'dp'), may hold values from 0.05 to 2
- tokens: bfloat16 [2, 2688, 8192], P('pipe', 'dp'), may hold values from -20 to 20
Outputs:
- new_master: float32 [2, 2, 8192, 256], P('pipe', None, 'dp')
- new_first: float32 [2, 2, 8192, 256], P('pipe', None, 'dp')
- new_second: float32 [2, 2, 8192, 256], P('pipe', None, 'dp')
- passed: bfloat16 [2, 2688, 1024], P('pipe', 'dp')
All inputs are finite; a program needn't handle non-finite values.
Results may differ from a plain program's by a relative error of at most 0.012.
The roundings to bfloat16 on the way count: a program that leaves them out, or rounds other values in their place, can miss the bound.
Values may be sent and summed in bfloat16 or wider, within the bound.
A program may use at most 64 MiB of HBM per device.

v0:
```python
import functools
import math

import jax
import jax.numpy as jnp
import numpy as np
from jax import lax
from jax.experimental import pallas as pl
from jax.experimental.pallas import tpu as pltpu
from jax.sharding import PartitionSpec as P

HEAD = 128
QH = 8
PIECE = 256
TURNED = 0
STEP = 10
WIDTH = QH * HEAD
MESH = pl.DeviceIdType.MESH


def adam(master, grads, first_moment, second_moment, clip):
    scaled = clip * grads
    new_first = 0.9 * first_moment + 0.1 * scaled
    new_second = 0.95 * second_moment + 0.05 * scaled * scaled
    step_mean = new_first / (1.0 - 0.9**STEP)
    step_var = new_second / (1.0 - 0.95**STEP)
    new_master = master - 0.003 * step_mean / (jnp.sqrt(step_var) + 1e-08)
    return new_master, new_first, new_second


def kernel(
    n_dp, n_pipe, count, turned,
    master, grads, first, second, tokens,
    new_master, new_first, new_second, passed,
    g_v, m_v, f_v, s_v, x_v, n_v, w, acc, part, slots, inv, kv, q_n,
    far_x, far_inv, far_kv,
    load_sem, own_sem, part_send, part_recv, z_send, y_send, c_send, w_recv,
    far_send, far_recv,
):
    me = lax.axis_index("dp")
    sec = lax.axis_index("pipe")
    total = n_dp * n_pipe
    lines, cores = 2, 2
    depth = n_dp // (lines * cores)
    core = lax.rem(me, cores)
    line = lax.rem(lax.div(me, cores), lines)
    z = lax.div(me, lines * cores)
    mine = (z, line, core)
    rows = g_v.shape[1]
    pieces = w_recv.shape[1]
    piece = rows // pieces
    dim = x_v.shape[1]
    seq = x_v.shape[0]

    def at(zz, yy, cc):
        return (zz * lines + yy) * cores + cc

    blocks = g_v.shape[0]
    states = ((master, m_v), (first, f_v), (second, s_v))
    loads = [
        pltpu.make_async_copy(grads.at[0], g_v, load_sem.at[0]),
        *[
            pltpu.make_async_copy(src.at[0, 0], dst.at[0], load_sem.at[1 + i])
            for i, (src, dst) in enumerate(states)
        ],
        pltpu.make_async_copy(tokens.at[0], x_v, load_sem.at[4]),
        *[
            pltpu.make_async_copy(
                src.at[0, pl.ds(1, blocks - 1)], dst.at[pl.ds(1, blocks - 1)], load_sem.at[5 + i]
            )
            for i, (src, dst) in enumerate(states)
        ],
    ]
    loads[0].start()

    flat = sec * n_dp + me

    def peer(k):
        other = lax.rem(flat + k, total)
        return {"dp": lax.rem(other, n_dp), "pipe": lax.div(other, n_dp)}

    barrier = pltpu.get_barrier_semaphore()

    @pl.loop(1, total)
    def _(k):
        pl.semaphore_signal(barrier, inc=1, device_id=peer(k), device_id_type=MESH)

    for load in loads[1:]:
        load.start()

    loads[0].wait()
    cols = g_v.shape[2]
    local = jnp.zeros((8, cols), jnp.float32)
    for b in range(blocks):
        g = g_v[b]
        local = local + jnp.sum((g * g).reshape(rows // 8, 8, cols), axis=0)
    lanes = local[:, :128]
    for i in range(1, cols // 128):
        lanes = lanes + local[:, i * 128 : (i + 1) * 128]
    part[...] = jnp.sum(lanes, axis=0, keepdims=True)

    pl.semaphore_wait(barrier, total - 1)

    own = pltpu.make_async_copy(part, slots.at[flat], part_recv)
    own.start()

    @pl.loop(1, total)
    def _(k):
        pltpu.make_async_remote_copy(
            src_ref=part, dst_ref=slots.at[flat], send_sem=part_send, recv_sem=part_recv,
            device_id=peer(k), device_id_type=MESH,
        ).start()

    after = lax.rem(sec + 1, n_pipe)

    def to_next(src, dst, i):
        return pltpu.make_async_remote_copy(
            src_ref=src, dst_ref=dst, send_sem=far_send.at[i], recv_sem=far_recv.at[i],
            device_id={"dp": me, "pipe": after}, device_id_type=MESH,
        )

    head_copy = to_next(tokens.at[0, :, pl.ds(0, WIDTH)], far_x, 0)

    loads[4].wait()
    step = 512

    def squares(i, carry):
        for j in range(step // 128):
            x = x_v[:, pl.ds(pl.multiple_of(i * step + j * 128, 128), 128)].astype(jnp.float32)
            carry = carry + x * x
        return carry

    sq = lax.fori_loop(0, dim // step, squares, jnp.zeros((seq, 128), jnp.float32))
    mean_sq = jnp.sum(sq, axis=1, keepdims=True) / dim
    inv[...] = jnp.broadcast_to(lax.rsqrt(mean_sq + 1e-06), (seq, 128))
    inv_copy = to_next(inv, far_inv, 1)
    inv_copy.start()

    @pl.loop(0, dim // step)
    def _(i):
        scale = inv[...]
        for j in range(step // 128):
            at_cols = pl.ds(pl.multiple_of(i * step + j * 128, 128), 128)
            n_v[:, at_cols] = (x_v[:, at_cols].astype(jnp.float32) * scale).astype(jnp.bfloat16)

    for load in loads[1:4]:
        load.wait()
    acc[...] = jnp.zeros_like(acc)

    pltpu.make_async_copy(slots, slots, part_recv).wait()
    summed = jnp.sum(slots[...], axis=0)
    square_sum = jnp.sum(summed, axis=1, keepdims=True)
    root = np.float32(0.5) * np.sqrt(np.float32(count))
    clip = jnp.minimum(1.0, root / jnp.sqrt(square_sum + 1e-06))

    def span(b, ch):
        return pl.ds(pl.multiple_of(at(*b) * rows + ch * piece, piece), piece)

    def send(b, ch, dst, sem):
        return pltpu.make_async_remote_copy(
            src_ref=w.at[span(b, ch)], dst_ref=w.at[span(b, ch)],
            send_sem=sem, recv_sem=w_recv.at[at(*b), ch],
            device_id={"dp": dst, "pipe": sec}, device_id_type=MESH,
        )

    def chip(b):
        return b[0]

    def up(b, ch, other=0):
        return send(b, ch, at(z + 1, line, core), z_send.at[0, other, chip(b), ch])

    def down(b, ch, other=0):
        return send(b, ch, at(z - 1, line, core), z_send.at[1, other, chip(b), ch])

    def across(b, ch):
        return send(b, ch, at(z, 1 - line, core), y_send.at[chip(b), ch])

    def beside(b, ch):
        return send(b, ch, at(z, line, 1 - core), c_send.at[b[0] * lines + b[1], ch])

    def arrived(b, ch):
        send(b, ch, me, c_send.at[0, 0]).wait_recv()

    def both_ways(b, ch, other=0):
        @pl.when(z < depth - 1)
        def _():
            up(b, ch, other).start()

        @pl.when(z > 0)
        def _():
            down(b, ch, other).start()

    whole_blocks = rows % 128 == 0

    def multiply(b):
        if whole_blocks:
            at_rows = pl.ds(pl.multiple_of(at(*b) * rows, rows), rows)
            acc[...] += jnp.dot(n_v[:, at_rows], w[at_rows, :], preferred_element_type=jnp.float32)

    def update(b, r):
        results = adam(m_v[b, r, :], g_v[b, r, :], f_v[b, r, :], s_v[b, r, :], clip)
        for ref, result in zip((new_master, new_first, new_second), results):
            ref[0, b, r, :] = result
        return results[0]

    def multiply_piece(b, ch):
        if whole_blocks:
            at_rows = span(b, ch)
            acc[...] += jnp.dot(n_v[:, at_rows], w[at_rows, :], preferred_element_type=jnp.float32)

    for ch in range(pieces):
        w[span(mine, ch), :] = update(0, pl.ds(ch * piece, piece)).astype(jnp.bfloat16)
        both_ways(mine, ch)
        across(mine, ch).start()
        beside(mine, ch).start()

    head_copy.start()
    multiply(mine)

    for ch in range(turned):
        b = (z, 1 - line, core)
        arrived(b, ch)
        both_ways(b, ch, 1)
        beside(b, ch).start()

    for t in range(depth):
        far = t + 1
        if far < depth:
            for other in (0, 1):
                for ch in range(pieces if other == 0 else turned):

                    def along(zz, onward, end):
                        b = (zz, (line, 1 - line)[other], core)
                        arrived(b, ch)

                        @pl.when(end)
                        def _():
                            onward(b, ch, other).start()

                        if other == 0 and ch >= turned:
                            across(b, ch).start()
                        beside(b, ch).start()

                    @pl.when(z - far >= 0)
                    def _():
                        along(z - far, up, z < depth - 1)

                    @pl.when(z + far < depth)
                    def _():
                        along(z + far, down, z > 0)

        def at_distance(visit):
            if t == 0:
                visit(z)
            else:

                @pl.when(z - t >= 0)
                def _():
                    visit(z - t)

                @pl.when(z + t < depth)
                def _():
                    visit(z + t)

        last = t == depth - 1
        if last:

            def use_own(zz):
                multiply((zz, line, core))
                b = (zz, line, 1 - core)
                for ch in range(pieces):
                    arrived(b, ch)
                multiply(b)

            at_distance(use_own)
        for ch in range(turned, pieces):

            def pass_on(zz):
                b = (zz, 1 - line, core)
                arrived(b, ch)
                beside(b, ch).start()
                if last:
                    multiply_piece(b, ch)

            at_distance(pass_on)

        def use(zz):
            if last:
                for ch in range(turned):
                    multiply_piece((zz, 1 - line, core), ch)
                b = (zz, 1 - line, 1 - core)
                for ch in range(pieces):
                    arrived(b, ch)
                    multiply_piece(b, ch)
                return
            if t > 0:
                multiply((zz, line, core))
            multiply((zz, 1 - line, core))
            for yy in (line, 1 - line):
                b = (zz, yy, 1 - core)
                for ch in range(pieces):
                    arrived(b, ch)
                multiply(b)

        if t == 0:
            for load in loads[5:]:
                load.wait()
            for b in range(1, blocks):
                for ch in range(pieces):
                    update(b, pl.ds(ch * piece, piece))
        if t == min(2, depth - 1):
            head_copy.wait_recv()
            inv_copy.wait_recv()
            for h in range(QH):
                hs = pl.ds(h * HEAD, HEAD)
                q_n[:, hs] = (far_x[:, hs].astype(jnp.float32) * far_inv[...]).astype(jnp.bfloat16)
        at_distance(use)

    if whole_blocks:
        projected = acc[...]
    else:

        def run(i, carry):
            d = pl.ds(pl.multiple_of(i * step, step), step)
            return carry + jnp.dot(n_v[:, d], w[d, :], preferred_element_type=jnp.float32)

        projected = lax.fori_loop(0, dim // step, run, acc[...])
    kv[...] = projected.astype(jnp.bfloat16)
    kv_copy = to_next(kv, far_kv, 2)
    kv_copy.start()
    row = lax.broadcasted_iota(jnp.int32, (seq, seq), 0)
    col = lax.broadcasted_iota(jnp.int32, (seq, seq), 1)
    causal = row >= col
    kv_copy.wait_recv()
    keys = far_kv[:, :HEAD]
    values = far_kv[:, HEAD:]
    for h in range(QH):
        hs = pl.ds(h * HEAD, HEAD)
        scores = lax.dot_general(
            q_n[:, hs], keys, (((1,), (1,)), ((), ())), preferred_element_type=jnp.float32
        ) * np.float32(1.0 / math.sqrt(HEAD))
        scores = jnp.where(causal, scores, -1e30)
        top = jnp.max(scores, axis=1, keepdims=True)
        expd = jnp.exp(scores - top)
        probs = (expd / jnp.sum(expd, axis=1, keepdims=True)).astype(jnp.bfloat16)
        attn = jnp.dot(probs, values, preferred_element_type=jnp.float32)
        passed[0, :, hs] = (far_x[:, hs].astype(jnp.float32) + attn).astype(jnp.bfloat16)

    for c in (head_copy, inv_copy, kv_copy):
        c.wait_send()
    pltpu.make_async_copy(
        slots.at[pl.ds(0, total - 1)], slots.at[pl.ds(0, total - 1)], part_send
    ).wait()
    for ch in range(pieces):
        for zz in range(depth):
            for other in range(2 if ch < turned else 1):
                b = (zz, (line, 1 - line)[other], core)

                @pl.when(jnp.logical_and(zz <= z, z < depth - 1))
                def _():
                    up(b, ch, other).wait_send()

                @pl.when(jnp.logical_and(zz >= z, z > 0))
                def _():
                    down(b, ch, other).wait_send()

            b = (zz, line, core)
            if ch >= turned:
                across(b, ch).wait_send()
            else:

                @pl.when(zz == z)
                def _():
                    across(b, ch).wait_send()

            for yy in range(lines):
                beside((zz, yy, core), ch).wait_send()


def write_out(*refs):
    half = (len(refs) - 1) // 2
    sems = refs[-1]
    copies = [
        pltpu.make_async_copy(refs[i], refs[half + i], sems.at[i]) for i in range(half)
    ]
    for c in copies:
        c.start()
    for c in copies:
        c.wait()


def on_device(n_dp, n_pipe, master, grads, first_moment, second_moment, tokens):
    _, blocks, rows, cols = master.shape
    _, seq, dim = tokens.shape
    total = n_dp * n_pipe
    count = grads.size * total
    pieces = max(1, rows // PIECE)
    depth = n_dp // 4
    f32, bf16 = jnp.float32, jnp.bfloat16
    hbm = pl.BlockSpec(memory_space=pltpu.HBM)
    vmem = pl.BlockSpec(memory_space=pltpu.VMEM)
    dma = pltpu.SemaphoreType.DMA
    shapes = (
        *[jax.ShapeDtypeStruct(master.shape, f32)] * 3,
        jax.ShapeDtypeStruct((1, seq, WIDTH), bf16),
    )
    master, grads, first_moment, second_moment, tokens = (
        pltpu.with_memory_space_constraint(v, pltpu.HBM)
        for v in (master, grads, first_moment, second_moment, tokens)
    )
    results = pl.pallas_call(
        functools.partial(kernel, n_dp, n_pipe, count, TURNED if pieces > TURNED else 0),
        out_shape=tuple(pltpu.VMEM(v.shape, v.dtype) for v in shapes),
        in_specs=[hbm] * 5,
        out_specs=(vmem,) * 4,
        scratch_shapes=[
            pltpu.VMEM((blocks, rows, cols), f32),
            pltpu.VMEM((blocks, rows, cols), f32),
            pltpu.VMEM((blocks, rows, cols), f32),
            pltpu.VMEM((blocks, rows, cols), f32),
            pltpu.VMEM((seq, dim), bf16),
            pltpu.VMEM((seq, dim), bf16),
            pltpu.VMEM((n_dp * rows, cols), bf16),
            pltpu.VMEM((seq, cols), f32),
            pltpu.VMEM((1, 128), f32),
            pltpu.VMEM((total, 1, 128), f32),
            pltpu.VMEM((seq, 128), f32),
            pltpu.VMEM((seq, cols), bf16),
            pltpu.VMEM((seq, WIDTH), bf16),
            pltpu.VMEM((seq, WIDTH), bf16),
            pltpu.VMEM((seq, 128), f32),
            pltpu.VMEM((seq, cols), bf16),
            dma((8,)),
            dma,
            dma,
            dma,
            dma((2, 2, depth, pieces)),
            dma((depth, pieces)),
            dma((n_dp // 2, pieces)),
            dma((n_dp, pieces)),
            dma((3,)),
            dma((3,)),
        ],
        compiler_params=pltpu.CompilerParams(
            collective_id=0, has_side_effects=True, vmem_limit_bytes=48 * 1024 * 1024
        ),
        name="section",
    )(master, grads, first_moment, second_moment, tokens)
    return pl.pallas_call(
        write_out,
        out_shape=shapes,
        in_specs=[vmem] * 4,
        out_specs=(hbm,) * 4,
        scratch_shapes=[dma((4,))],
        compiler_params=pltpu.CompilerParams(vmem_limit_bytes=1024 * 1024),
        name="write_out",
    )(*results)


def solution(mesh):
    split = P("pipe", None, "dp", None)
    rows = P("pipe", "dp", None)
    return jax.shard_map(
        functools.partial(on_device, mesh.shape["dp"], mesh.shape["pipe"]),
        mesh=mesh,
        in_specs=(split, split, split, split, rows),
        out_specs=(split, split, split, rows),
        check_vma=False,
    )
```

profile of v0, /device:TPU:0, one launch (start us, length us, event | category | flops | bytes accessed | tf_op | source)
XLA Modules:
  0.0 44.4 jit_solution(10916486328362797739)
XLA Ops:
  0.6 41.9 %section.1 = (f32[1,2,512,256]{3,2,1,0:T(8,128)S(1)}, f32[1,2,512,256]{3,2,1,0:T(8,128)S(1)}, f32[1,2,512,256]{3,2,1,0:T(8,128)S(1)}, bf16[1,168,1024]{2,1,0:T(8,128)(2,1)S(1)}) custom-call(f32[1,2,512,256]{3,2,1,0:T(8,128)} %master.1, f32[1,2,512,256]{3,2,1,0:T(8,128)} %grads.1, f32[1,2,512,256]{3,2,1,0:T(8,128)} %first.1, f32[1,2,512,256]{3,2,1,0:T(8,128)} %second.1, ...), custom_call_target="tpu_custom_call" | custom-call | tf_op jit(solution)/shard_map/section/pallas_call | solution.py:411
  42.6 1.8 %write_out.1 = (f32[1,2,512,256]{3,2,1,0:T(8,128)}, f32[1,2,512,256]{3,2,1,0:T(8,128)}, f32[1,2,512,256]{3,2,1,0:T(8,128)}, bf16[1,168,1024]{2,1,0:T(8,128)(2,1)}) custom-call(f32[1,2,512,256]{3,2,1,0:T(8,128)S(1)} %get-tuple-element.8.refs_0_, f32[1,2,512,256]{3,2,1,0:T(8,128)S(1)} %get-tuple-element.9.refs_1_, ...), custom_call_target="tpu_custom_call" | custom-call | tf_op jit(solution)/shard_map/write_out/pallas_call | solution.py:449
where the time goes:
time: 44.5 us; the launch traced here: 44.4 us
  Pallas kernels  43.7 us (98%)
  between operations  0.64 us (1%)
    pallas_call x1, Pallas kernels, on_device(): pl.pallas_call(functools.partial(kernel, n_dp, n_pipe, count, TURNED if p...  41.9 us
    pallas_call x1, Pallas kernels, on_device(): pl.pallas_call(write_out, out_shape=shapes, in_specs=[vmem] * 4, out_spec...  1.8 us

commit v1 on v0

--- a/solution.py
+++ b/solution.py
@@ -13,6 +13,8 @@
 QH = 8
 PIECE = 256
 TURNED = 0
+CHUNK = 128
+PAIR_TURNED = 1
 STEP = 10
 WIDTH = QH * HEAD
 MESH = pl.DeviceIdType.MESH
@@ -377,6 +379,460 @@
                 beside((zz, yy, core), ch).wait_send()
 
 
+def paired(
+    n_dp, n_pipe, count, turned,
+    master, grads, first, second, tokens,
+    new_master, new_first, new_second, passed,
+    g_v, m_v, f_v, s_v, x_v, n_v, w, acc_k, acc_v, part, slots, sums, inv, kv, q_n, probs,
+    far_x, far_inv, far_kv,
+    load_sem, part_send, part_recv, sum_send, sum_recv, ready, p_send, q_send, y_send, c_send,
+    w_recv, far_send, far_recv,
+):
+    me = lax.axis_index("dp")
+    sec = lax.axis_index("pipe")
+    lines, cores, depth = 2, 2, 4
+    group = n_pipe * lines * cores
+    core = lax.rem(me, cores)
+    line = lax.rem(lax.div(me, cores), lines)
+    z = lax.div(me, lines * cores)
+    seat = sec * lines * cores + lax.rem(me, lines * cores)
+    upper = lax.div(z, 2)
+    inner = jnp.logical_or(z == 1, z == 2)
+    outer = jnp.logical_not(inner)
+    planes = (z, 1 - z + 4 * upper, 2 - upper, 3 - 3 * upper)
+    blocks, rows, cols = g_v.shape
+    seq, dim = x_v.shape
+    chunk = CHUNK
+    chunks = rows // chunk
+    units = [(h, c) for h in range(2) for c in range(chunks)]
+    straight = [u for u in units if u[0] == 0 or u[1] >= turned]
+    turns = [(1, c) for c in range(turned)]
+
+    def at(zz, yy, cc):
+        return (zz * lines + yy) * cores + cc
+
+    def device(zz, r):
+        return {"dp": zz * lines * cores + lax.rem(r, lines * cores), "pipe": lax.div(r, lines * cores)}
+
+    states = ((master, m_v), (first, f_v), (second, s_v))
+    loads = [
+        pltpu.make_async_copy(grads.at[0], g_v, load_sem.at[0]),
+        *[
+            pltpu.make_async_copy(src.at[0, 0], dst.at[0], load_sem.at[1 + i])
+            for i, (src, dst) in enumerate(states)
+        ],
+        pltpu.make_async_copy(tokens.at[0], x_v, load_sem.at[4]),
+        *[
+            pltpu.make_async_copy(
+                src.at[0, pl.ds(1, blocks - 1)], dst.at[pl.ds(1, blocks - 1)], load_sem.at[5 + i]
+            )
+            for i, (src, dst) in enumerate(states)
+        ],
+    ]
+    loads[0].start()
+    barrier = pltpu.get_barrier_semaphore()
+
+    @pl.loop(1, group)
+    def _(k):
+        pl.semaphore_signal(
+            barrier, inc=1, device_id=device(z, lax.rem(seat + k, group)), device_id_type=MESH
+        )
+
+    @pl.loop(0, group * (depth - 1 - z))
+    def _(k):
+        pl.semaphore_signal(
+            barrier, inc=1, device_id=device(z + 1 + lax.div(k, group), lax.rem(k, group)),
+            device_id_type=MESH,
+        )
+
+    loads[4].start()
+    for load in loads[1:4] + loads[5:]:
+        load.start()
+
+    for k in range(depth):
+
+        @pl.when(z == k)
+        def _():
+            pl.semaphore_wait(barrier, group - 1 + group * k)
+
+    @pl.loop(0, z)
+    def _(zz):
+        pl.semaphore_signal(
+            ready.at[z], inc=1, device_id=device(zz, seat), device_id_type=MESH
+        )
+
+    loads[0].wait()
+    local = jnp.zeros((8, cols), jnp.float32)
+    for b in range(blocks):
+        g = g_v[b]
+        local = local + jnp.sum((g * g).reshape(rows // 8, 8, cols), axis=0)
+    lanes = local[:, :128]
+    for i in range(1, cols // 128):
+        lanes = lanes + local[:, i * 128 : (i + 1) * 128]
+    part[...] = jnp.sum(lanes, axis=0, keepdims=True)
+
+
+    def give(zz, r):
+        return pltpu.make_async_remote_copy(
+            src_ref=part, dst_ref=slots.at[z * group + seat], send_sem=part_send,
+            recv_sem=part_recv.at[z], device_id=device(zz, r), device_id_type=MESH,
+        )
+
+    own = pltpu.make_async_copy(part, slots.at[z * group + seat], part_recv.at[z])
+    own.start()
+
+    @pl.loop(0, group * z)
+    def _(k):
+        give(lax.div(k, group), lax.rem(k, group)).start()
+
+    @pl.loop(1, group)
+    def _(k):
+        give(z, lax.rem(seat + k, group)).start()
+
+    after = lax.rem(sec + 1, n_pipe)
+
+    def to_next(src, dst, i):
+        return pltpu.make_async_remote_copy(
+            src_ref=src, dst_ref=dst, send_sem=far_send.at[i], recv_sem=far_recv.at[i],
+            device_id={"dp": me, "pipe": after}, device_id_type=MESH,
+        )
+
+    head_copy = to_next(tokens.at[0, :, pl.ds(0, WIDTH)], far_x, 0)
+
+    loads[4].wait()
+    step = 512
+
+    def squares(i, carry):
+        for j in range(step // 128):
+            x = x_v[:, pl.ds(pl.multiple_of(i * step + j * 128, 128), 128)].astype(jnp.float32)
+            carry = carry + x * x
+        return carry
+
+    sq = lax.fori_loop(0, dim // step, squares, jnp.zeros((seq, 128), jnp.float32))
+    mean_sq = jnp.sum(sq, axis=1, keepdims=True) / dim
+    inv[...] = jnp.broadcast_to(lax.rsqrt(mean_sq + 1e-06), (seq, 128))
+    inv_copy = to_next(inv, far_inv, 1)
+
+
+    @pl.loop(0, dim // step)
+    def _(i):
+        scale = inv[...]
+        for j in range(step // 128):
+            at_cols = pl.ds(pl.multiple_of(i * step + j * 128, 128), 128)
+            n_v[:, at_cols] = (x_v[:, at_cols].astype(jnp.float32) * scale).astype(jnp.bfloat16)
+
+    acc_k[...] = jnp.zeros_like(acc_k)
+    acc_v[...] = jnp.zeros_like(acc_v)
+
+    def plane_slots(zz):
+        return slots.at[pl.ds(zz * group, group)]
+
+    def plane_wait(zz):
+        pltpu.make_async_copy(plane_slots(zz), plane_slots(zz), part_recv.at[zz]).wait()
+
+    plane_wait(z)
+    sums[z] = jnp.sum(plane_slots(z)[...], axis=0)
+
+    def lift(zz):
+        return pltpu.make_async_remote_copy(
+            src_ref=sums.at[z], dst_ref=sums.at[z], send_sem=sum_send.at[zz],
+            recv_sem=sum_recv.at[z], device_id=device(zz, seat), device_id_type=MESH,
+        )
+
+    for zz in range(1, depth):
+
+        @pl.when(z < zz)
+        def _():
+            pl.semaphore_wait(ready.at[zz], 1)
+            lift(zz).start()
+
+    for load in loads[1:4]:
+        load.wait()
+    for zz in range(depth):
+
+        @pl.when(zz > z)
+        def _():
+            plane_wait(zz)
+            sums[zz] = jnp.sum(plane_slots(zz)[...], axis=0)
+
+        @pl.when(zz < z)
+        def _():
+            pltpu.make_async_copy(sums.at[zz], sums.at[zz], sum_recv.at[zz]).wait()
+
+    square_sum = jnp.sum(jnp.sum(sums[...], axis=0), axis=1, keepdims=True)
+    root = np.float32(0.5) * np.sqrt(np.float32(count))
+    clip = jnp.minimum(1.0, root / jnp.sqrt(square_sum + 1e-06))
+
+    def send(b, u, dst, sem):
+        h, c = u
+        here = w.at[h, pl.ds(pl.multiple_of(at(*b) * rows + c * chunk, chunk), chunk)]
+        return pltpu.make_async_remote_copy(
+            src_ref=here, dst_ref=here, send_sem=sem, recv_sem=w_recv.at[h, at(*b), c],
+            device_id={"dp": dst, "pipe": sec}, device_id_type=MESH,
+        )
+
+    beyond = jnp.where(z == 1, 2, 1)
+
+    def to_pair(b, u):
+        send(b, u, at(planes[1], line, core), p_send).start()
+
+    def to_beyond(b, u):
+        send(b, u, at(beyond, line, core), q_send).start()
+
+    def across(b, u):
+        send(b, u, at(z, 1 - line, core), y_send).start()
+
+    def beside(b, u):
+        send(b, u, at(z, line, 1 - core), c_send).start()
+
+    def arrived(b, u):
+        send(b, u, me, c_send).wait_recv()
+
+    def here(s):
+        return (planes[s], line, core)
+
+    def there(s):
+        return (planes[s], 1 - line, core)
+
+    def update(b, r, hs):
+        results = adam(m_v[b, r, hs], g_v[b, r, hs], f_v[b, r, hs], s_v[b, r, hs], clip)
+        for ref, result in zip((new_master, new_first, new_second), results):
+            ref[0, b, r, hs] = result
+        return results[0]
+
+    def product(h, zz, yy, cc, low=0, high=None):
+        size = (rows if high is None else high) - low
+        d = pl.ds(pl.multiple_of(at(zz, yy, cc) * rows + low, 128), size)
+        acc = (acc_k, acc_v)[h]
+        acc[...] += jnp.dot(n_v[:, d], w[h, d, :], preferred_element_type=jnp.float32)
+
+    def multiply(s, h):
+        @pl.loop(0, cores)
+        def _(cc):
+            product(h, planes[s], line, cc)
+            product(h, planes[s], 1 - line, cc, turned * chunk if h and s else 0)
+
+    def from_beside(s, own_units, other_units):
+        for u in own_units:
+            arrived((planes[s], line, 1 - core), u)
+        for u in other_units:
+            arrived((planes[s], 1 - line, 1 - core), u)
+
+    for h, c in units:
+        r = pl.ds(c * chunk, chunk)
+        w[h, pl.ds(pl.multiple_of(me * rows + c * chunk, chunk), chunk), :] = update(
+            0, r, slice(h * HEAD, (h + 1) * HEAD)
+        ).astype(jnp.bfloat16)
+        u = (h, c)
+        to_pair(here(0), u)
+
+        @pl.when(inner)
+        def _():
+            to_beyond(here(0), u)
+
+        across(here(0), u)
+        beside(here(0), u)
+
+    head_copy.start()
+    inv_copy.start()
+    for load in loads[5:]:
+        load.wait()
+    for b in range(1, blocks):
+        for c in range(chunks):
+            for h in range(2):
+                update(b, pl.ds(c * chunk, chunk), slice(h * HEAD, (h + 1) * HEAD))
+
+    for u in units:
+        arrived(here(1), u)
+
+        @pl.when(inner)
+        def _():
+            to_beyond(here(1), u)
+            arrived(here(2), u)
+            to_pair(here(2), u)
+            beside(here(2), u)
+
+        if u in straight:
+            across(here(1), u)
+        beside(here(1), u)
+        arrived(there(0), u)
+        beside(there(0), u)
+
+    @pl.when(inner)
+    def _():
+        for u in straight:
+            across(here(2), u)
+        for u in turns:
+            to_beyond(there(0), u)
+
+    @pl.when(outer)
+    def _():
+        for u in turns:
+            to_pair(there(0), u)
+
+    from_beside(0, units, units)
+    multiply(0, 0)
+    multiply(0, 1)
+
+    for u in units:
+
+        @pl.when(inner)
+        def _():
+            arrived(here(3), u)
+            to_pair(here(3), u)
+            across(here(3), u) if u in straight else None
+            beside(here(3), u)
+
+        @pl.when(outer)
+        def _():
+            arrived(here(2), u)
+            across(here(2), u) if u in straight else None
+            beside(here(2), u)
+
+        if u in straight:
+            arrived(there(1), u)
+            beside(there(1), u)
+
+    @pl.when(inner)
+    def _():
+        for u in turns:
+            arrived(there(1), u)
+            to_beyond(there(1), u)
+            beside(there(1), u)
+            to_pair(there(0), u)
+        for s in (2, 3):
+            for u in turns:
+                arrived(there(s), u)
+                to_pair(there(s), u)
+                beside(there(s), u)
+
+    from_beside(1, units, straight)
+    multiply(1, 0)
+    multiply(1, 1)
+    head_copy.wait_recv()
+    inv_copy.wait_recv()
+    for h in range(QH):
+        hs = pl.ds(h * HEAD, HEAD)
+        q_n[:, hs] = (far_x[:, hs].astype(jnp.float32) * far_inv[...]).astype(jnp.bfloat16)
+
+    for u in units:
+
+        @pl.when(outer)
+        def _():
+            arrived(here(3), u)
+            across(here(3), u) if u in straight else None
+            beside(here(3), u)
+
+        if u in straight:
+            arrived(there(2), u)
+            beside(there(2), u)
+
+    from_beside(2, units, straight)
+    multiply(2, 0)
+    multiply(2, 1)
+
+    for u in straight:
+        if u[0] == 0:
+            arrived(there(3), u)
+            beside(there(3), u)
+    from_beside(3, [u for u in units if u[0] == 0], [u for u in straight if u[0] == 0])
+    multiply(3, 0)
+    kv[0] = acc_k[...].astype(jnp.bfloat16)
+    k_copy = to_next(kv.at[0], far_kv.at[0], 2)
+    k_copy.start()
+    for u in units:
+        if u[0] == 1:
+            arrived((planes[3], line, 1 - core), u)
+    for cc in range(cores):
+        product(1, planes[3], line, cc)
+    last = [u for u in straight if u[0] == 1]
+    for u in last:
+        arrived(there(3), u)
+        beside(there(3), u)
+
+    @pl.when(outer)
+    def _():
+        for s in (1, 2, 3):
+            for u in turns:
+                arrived(there(s), u)
+                beside(there(s), u)
+
+    for u in last:
+        arrived((planes[3], 1 - line, 1 - core), u)
+
+    @pl.loop(0, cores)
+    def _(cc):
+        product(1, planes[3], 1 - line, cc, turned * chunk)
+
+    if turned:
+        for s in (1, 2, 3):
+            for u in turns:
+                arrived((planes[s], 1 - line, 1 - core), u)
+        for s in (1, 2, 3):
+
+            @pl.loop(0, cores)
+            def _(cc):
+                product(1, planes[s], 1 - line, cc, 0, turned * chunk)
+
+    kv[1] = acc_v[...].astype(jnp.bfloat16)
+    v_copy = to_next(kv.at[1], far_kv.at[1], 3)
+    v_copy.start()
+    row = lax.broadcasted_iota(jnp.int32, (seq, seq), 0)
+    col = lax.broadcasted_iota(jnp.int32, (seq, seq), 1)
+    causal = row >= col
+    k_copy.wait_recv()
+    keys = far_kv[0]
+    for h in range(QH):
+        hs = pl.ds(h * HEAD, HEAD)
+        scores = lax.dot_general(
+            q_n[:, hs], keys, (((1,), (1,)), ((), ())), preferred_element_type=jnp.float32
+        ) * np.float32(1.0 / math.sqrt(HEAD))
+        scores = jnp.where(causal, scores, -1e30)
+        top = jnp.max(scores, axis=1, keepdims=True)
+        expd = jnp.exp(scores - top)
+        probs[h] = (expd / jnp.sum(expd, axis=1, keepdims=True)).astype(jnp.bfloat16)
+    v_copy.wait_recv()
+    values = far_kv[1]
+    for h in range(QH):
+        hs = pl.ds(h * HEAD, HEAD)
+        attn = jnp.dot(probs[h], values, preferred_element_type=jnp.float32)
+        passed[0, :, hs] = (far_x[:, hs].astype(jnp.float32) + attn).astype(jnp.bfloat16)
+
+    for c in (head_copy, inv_copy, k_copy, v_copy):
+        c.wait_send()
+
+    for k in range(depth):
+
+        @pl.when(z == k)
+        def _():
+            sent = slots.at[pl.ds(0, group - 1 + group * k)]
+            pltpu.make_async_copy(sent, sent, part_send).wait()
+
+    for zz in range(1, depth):
+
+        @pl.when(z < zz)
+        def _():
+            lift(zz).wait_send()
+
+    def sent(n, sem):
+        span = w.at[0, pl.ds(0, n * chunk)]
+        pltpu.make_async_copy(span, span, sem).wait()
+
+    n, t = len(units), len(turns)
+
+    @pl.when(inner)
+    def _():
+        sent(3 * (n + t), p_send)
+        sent(2 * (n + t), q_send)
+
+    @pl.when(outer)
+    def _():
+        sent(n + t, p_send)
+
+    sent(n + 3 * len(straight), y_send)
+    sent(8 * n, c_send)
+
+
 def write_out(*refs):
     half = (len(refs) - 1) // 2
     sems = refs[-1]
@@ -395,7 +851,6 @@
     total = n_dp * n_pipe
     count = grads.size * total
     pieces = max(1, rows // PIECE)
-    depth = n_dp // 4
     f32, bf16 = jnp.float32, jnp.bfloat16
     hbm = pl.BlockSpec(memory_space=pltpu.HBM)
     vmem = pl.BlockSpec(memory_space=pltpu.VMEM)
@@ -408,12 +863,44 @@
         pltpu.with_memory_space_constraint(v, pltpu.HBM)
         for v in (master, grads, first_moment, second_moment, tokens)
     )
-    results = pl.pallas_call(
-        functools.partial(kernel, n_dp, n_pipe, count, TURNED if pieces > TURNED else 0),
-        out_shape=tuple(pltpu.VMEM(v.shape, v.dtype) for v in shapes),
-        in_specs=[hbm] * 5,
-        out_specs=(vmem,) * 4,
-        scratch_shapes=[
+    depth = n_dp // 4
+    if depth == 4 and rows % CHUNK == 0 and cols == 2 * HEAD:
+        turned = PAIR_TURNED if rows // CHUNK > PAIR_TURNED else 0
+        body = functools.partial(paired, n_dp, n_pipe, count, turned)
+        scratch = [
+            *[pltpu.VMEM((blocks, rows, cols), f32)] * 4,
+            pltpu.VMEM((seq, dim), bf16),
+            pltpu.VMEM((seq, dim), bf16),
+            pltpu.VMEM((2, n_dp * rows, HEAD), bf16),
+            pltpu.VMEM((seq, HEAD), f32),
+            pltpu.VMEM((seq, HEAD), f32),
+            pltpu.VMEM((1, 128), f32),
+            pltpu.VMEM((total, 1, 128), f32),
+            pltpu.VMEM((depth, 1, 128), f32),
+            pltpu.VMEM((seq, 128), f32),
+            pltpu.VMEM((2, seq, HEAD), bf16),
+            pltpu.VMEM((seq, WIDTH), bf16),
+            pltpu.VMEM((QH, seq, seq), bf16),
+            pltpu.VMEM((seq, WIDTH), bf16),
+            pltpu.VMEM((seq, 128), f32),
+            pltpu.VMEM((2, seq, HEAD), bf16),
+            dma((8,)),
+            dma,
+            dma((depth,)),
+            dma((depth,)),
+            dma((depth,)),
+            pltpu.SemaphoreType.REGULAR((depth,)),
+            dma,
+            dma,
+            dma,
+            dma,
+            dma((2, n_dp, rows // CHUNK)),
+            dma((4,)),
+            dma((4,)),
+        ]
+    else:
+        body = functools.partial(kernel, n_dp, n_pipe, count, TURNED if pieces > TURNED else 0)
+        scratch = [
             pltpu.VMEM((blocks, rows, cols), f32),
             pltpu.VMEM((blocks, rows, cols), f32),
             pltpu.VMEM((blocks, rows, cols), f32),
@@ -440,7 +927,13 @@
             dma((n_dp, pieces)),
             dma((3,)),
             dma((3,)),
-        ],
+        ]
+    results = pl.pallas_call(
+        body,
+        out_shape=tuple(pltpu.VMEM(v.shape, v.dtype) for v in shapes),
+        in_specs=[hbm] * 5,
+        out_specs=(vmem,) * 4,
+        scratch_shapes=scratch,
         compiler_params=pltpu.CompilerParams(
             collective_id=0, has_side_effects=True, vmem_limit_bytes=48 * 1024 * 1024
         ),

time: 44.5 us -> 42.4 us (0.953)
  Pallas kernels: 43.7 us -> 41.6 us
    pallas_call x1, Pallas kernels: 41.9 us -> 39.8 us  [on_device(): pl.pallas_call(body, out_shape=tuple((pltpu.VMEM(v.shape, v.dtype) for v...]
where the time goes in v1:
time: 42.4 us; the launch traced here: 42.2 us
  Pallas kernels  41.6 us (98%)
  between operations  0.64 us (2%)
    pallas_call x1, Pallas kernels, on_device(): pl.pallas_call(body, out_shape=tuple((pltpu.VMEM(v.shape, v.dtype) for v...  39.8 us
    pallas_call x1, Pallas kernels, on_device(): pl.pallas_call(write_out, out_shape=shapes, in_specs=[vmem] * 4, out_spec...  1.8 us

profile of v1, /device:TPU:0, one launch (start us, length us, event | category | flops | bytes accessed | tf_op | source)
XLA Modules:
  0.0 42.2 jit_solution(9535336331161167224)
XLA Ops:
  0.6 39.8 %section.1 = (f32[1,2,512,256]{3,2,1,0:T(8,128)S(1)}, f32[1,2,512,256]{3,2,1,0:T(8,128)S(1)}, f32[1,2,512,256]{3,2,1,0:T(8,128)S(1)}, bf16[1,168,1024]{2,1,0:T(8,128)(2,1)S(1)}) custom-call(f32[1,2,512,256]{3,2,1,0:T(8,128)} %master.1, f32[1,2,512,256]{3,2,1,0:T(8,128)} %grads.1, f32[1,2,512,256]{3,2,1,0:T(8,128)} %first.1, f32[1,2,512,256]{3,2,1,0:T(8,128)} %second.1, ...), custom_call_target="tpu_custom_call" | custom-call | tf_op jit(solution)/shard_map/section/pallas_call | solution.py:931
  40.4 1.8 %write_out.1 = (f32[1,2,512,256]{3,2,1,0:T(8,128)}, f32[1,2,512,256]{3,2,1,0:T(8,128)}, f32[1,2,512,256]{3,2,1,0:T(8,128)}, bf16[1,168,1024]{2,1,0:T(8,128)(2,1)}) custom-call(f32[1,2,512,256]{3,2,1,0:T(8,128)S(1)} %get-tuple-element.8.refs_0_, f32[1,2,512,256]{3,2,1,0:T(8,128)S(1)} %get-tuple-element.9.refs_1_, ...), custom_call_target="tpu_custom_call" | custom-call | tf_op jit(solution)/shard_map/write_out/pallas_call | solution.py:942

commit v2 on v1

--- a/solution.py
+++ b/solution.py
@@ -383,7 +383,7 @@
     n_dp, n_pipe, count, turned,
     master, grads, first, second, tokens,
     new_master, new_first, new_second, passed,
-    g_v, m_v, f_v, s_v, x_v, n_v, w, acc_k, acc_v, part, slots, sums, inv, kv, q_n, probs,
+    g_v, m_v, f_v, s_v, x_v, n_v, w, acc, part, slots, sums, inv, kv, q_n, probs,
     far_x, far_inv, far_kv,
     load_sem, part_send, part_recv, sum_send, sum_recv, ready, p_send, q_send, y_send, c_send,
     w_recv, far_send, far_recv,
@@ -521,8 +521,7 @@
             at_cols = pl.ds(pl.multiple_of(i * step + j * 128, 128), 128)
             n_v[:, at_cols] = (x_v[:, at_cols].astype(jnp.float32) * scale).astype(jnp.bfloat16)
 
-    acc_k[...] = jnp.zeros_like(acc_k)
-    acc_v[...] = jnp.zeros_like(acc_v)
+    acc[...] = jnp.zeros_like(acc)
 
     def plane_slots(zz):
         return slots.at[pl.ds(zz * group, group)]
@@ -600,17 +599,25 @@
             ref[0, b, r, hs] = result
         return results[0]
 
-    def product(h, zz, yy, cc, low=0, high=None):
-        size = (rows if high is None else high) - low
-        d = pl.ds(pl.multiple_of(at(zz, yy, cc) * rows + low, 128), size)
-        acc = (acc_k, acc_v)[h]
-        acc[...] += jnp.dot(n_v[:, d], w[h, d, :], preferred_element_type=jnp.float32)
-
-    def multiply(s, h):
-        @pl.loop(0, cores)
-        def _(cc):
-            product(h, planes[s], line, cc)
-            product(h, planes[s], 1 - line, cc, turned * chunk if h and s else 0)
+    halves = (slice(0, HEAD), slice(HEAD, 2 * HEAD))
+
+    def product(h, s, yy, cc, low, size):
+        d = pl.ds(pl.multiple_of(at(planes[s], yy, cc) * rows + low, 128), size)
+        return jnp.dot(n_v[:, d], w[h, d, :], preferred_element_type=jnp.float32)
+
+    def product_line(s, yy, h=None):
+        d = pl.ds(pl.multiple_of(at(planes[s], yy, 0) * rows, rows), cores * rows)
+        own = w[h, d, :] if h is not None else jnp.concatenate([w[0, d, :], w[1, d, :]], axis=1)
+        return jnp.dot(n_v[:, d], own, preferred_element_type=jnp.float32)
+
+    def straight_values(s):
+        low = turned * chunk
+        return product(1, s, 1 - line, 0, low, rows - low) + product(1, s, 1 - line, 1, low, rows - low)
+
+    def multiply(s):
+        acc[...] += product_line(s, line)
+        acc[:, halves[0]] += product_line(s, 1 - line, 0)
+        acc[:, halves[1]] += straight_values(s)
 
     def from_beside(s, own_units, other_units):
         for u in own_units:
@@ -671,8 +678,7 @@
             to_pair(there(0), u)
 
     from_beside(0, units, units)
-    multiply(0, 0)
-    multiply(0, 1)
+    acc[...] += product_line(0, line) + product_line(0, 1 - line)
 
     for u in units:
 
@@ -707,8 +713,7 @@
                 beside(there(s), u)
 
     from_beside(1, units, straight)
-    multiply(1, 0)
-    multiply(1, 1)
+    multiply(1)
     head_copy.wait_recv()
     inv_copy.wait_recv()
     for h in range(QH):
@@ -728,53 +733,46 @@
             beside(there(2), u)
 
     from_beside(2, units, straight)
-    multiply(2, 0)
-    multiply(2, 1)
-
+    multiply(2)
+
+    from_beside(3, [u for u in units if u[0] == 0], [])
+    acc[:, halves[0]] += product_line(3, line, 0)
     for u in straight:
         if u[0] == 0:
             arrived(there(3), u)
             beside(there(3), u)
-    from_beside(3, [u for u in units if u[0] == 0], [u for u in straight if u[0] == 0])
-    multiply(3, 0)
-    kv[0] = acc_k[...].astype(jnp.bfloat16)
+    from_beside(3, [], [u for u in units if u[0] == 0])
+    kv[0] = (acc[:, halves[0]] + product_line(3, 1 - line, 0)).astype(jnp.bfloat16)
     k_copy = to_next(kv.at[0], far_kv.at[0], 2)
     k_copy.start()
-    for u in units:
-        if u[0] == 1:
-            arrived((planes[3], line, 1 - core), u)
-    for cc in range(cores):
-        product(1, planes[3], line, cc)
+    from_beside(3, [u for u in units if u[0] == 1], [])
+    acc[:, halves[1]] += product_line(3, line, 1)
     last = [u for u in straight if u[0] == 1]
-    for u in last:
+
+    def turns_here():
+        @pl.when(outer)
+        def _():
+            for s in (1, 2, 3):
+                for u in turns:
+                    arrived(there(s), u)
+                    beside(there(s), u)
+
+    for u in last[:-1]:
         arrived(there(3), u)
         beside(there(3), u)
-
-    @pl.when(outer)
-    def _():
-        for s in (1, 2, 3):
-            for u in turns:
-                arrived(there(s), u)
-                beside(there(s), u)
-
-    for u in last:
-        arrived((planes[3], 1 - line, 1 - core), u)
-
-    @pl.loop(0, cores)
-    def _(cc):
-        product(1, planes[3], 1 - line, cc, turned * chunk)
-
+    turns_here()
+    arrived(there(3), last[-1])
+    beside(there(3), last[-1])
     if turned:
         for s in (1, 2, 3):
             for u in turns:
                 arrived((planes[s], 1 - line, 1 - core), u)
-        for s in (1, 2, 3):
-
-            @pl.loop(0, cores)
-            def _(cc):
-                product(1, planes[s], 1 - line, cc, 0, turned * chunk)
-
-    kv[1] = acc_v[...].astype(jnp.bfloat16)
+        acc[:, halves[1]] += sum(
+            product(1, s, 1 - line, cc, 0, turned * chunk) for s in (1, 2, 3) for cc in range(cores)
+        )
+    for u in last:
+        arrived((planes[3], 1 - line, 1 - core), u)
+    kv[1] = (acc[:, halves[1]] + straight_values(3)).astype(jnp.bfloat16)
     v_copy = to_next(kv.at[1], far_kv.at[1], 3)
     v_copy.start()
     row = lax.broadcasted_iota(jnp.int32, (seq, seq), 0)
@@ -872,8 +870,7 @@
             pltpu.VMEM((seq, dim), bf16),
             pltpu.VMEM((seq, dim), bf16),
             pltpu.VMEM((2, n_dp * rows, HEAD), bf16),
-            pltpu.VMEM((seq, HEAD), f32),
-            pltpu.VMEM((seq, HEAD), f32),
+            pltpu.VMEM((seq, cols), f32),
             pltpu.VMEM((1, 128), f32),
             pltpu.VMEM((total, 1, 128), f32),
             pltpu.VMEM((depth, 1, 128), f32),

time: 42.4 us -> 41.5 us (0.979)
  Pallas kernels: 41.6 us -> 40.7 us
    pallas_call x1, Pallas kernels: 39.8 us -> 38.9 us  [on_device(): pl.pallas_call(body, out_shape=tuple((pltpu.VMEM(v.shape, v.dtype) for v...]
where the time goes in v2:
time: 41.5 us; the launch traced here: 41.3 us
  Pallas kernels  40.7 us (98%)
  between operations  0.64 us (2%)
    pallas_call x1, Pallas kernels, on_device(): pl.pallas_call(body, out_shape=tuple((pltpu.VMEM(v.shape, v.dtype) for v...  38.9 us
    pallas_call x1, Pallas kernels, on_device(): pl.pallas_call(write_out, out_shape=shapes, in_specs=[vmem] * 4, out_spec...  1.8 us

profile of v2, /device:TPU:0, one launch (start us, length us, event | category | flops | bytes accessed | tf_op | source)
XLA Modules:
  0.0 41.3 jit_solution(7245603495332165103)
XLA Ops:
  0.6 38.9 %section.1 = (f32[1,2,512,256]{3,2,1,0:T(8,128)S(1)}, f32[1,2,512,256]{3,2,1,0:T(8,128)S(1)}, f32[1,2,512,256]{3,2,1,0:T(8,128)S(1)}, bf16[1,168,1024]{2,1,0:T(8,128)(2,1)S(1)}) custom-call(f32[1,2,512,256]{3,2,1,0:T(8,128)} %master.1, f32[1,2,512,256]{3,2,1,0:T(8,128)} %grads.1, f32[1,2,512,256]{3,2,1,0:T(8,128)} %first.1, f32[1,2,512,256]{3,2,1,0:T(8,128)} %second.1, ...), custom_call_target="tpu_custom_call" | custom-call | tf_op jit(solution)/shard_map/section/pallas_call | solution.py:928
  39.5 1.8 %write_out.1 = (f32[1,2,512,256]{3,2,1,0:T(8,128)}, f32[1,2,512,256]{3,2,1,0:T(8,128)}, f32[1,2,512,256]{3,2,1,0:T(8,128)}, bf16[1,168,1024]{2,1,0:T(8,128)(2,1)}) custom-call(f32[1,2,512,256]{3,2,1,0:T(8,128)S(1)} %get-tuple-element.8.refs_0_, f32[1,2,512,256]{3,2,1,0:T(8,128)S(1)} %get-tuple-element.9.refs_1_, ...), custom_call_target="tpu_custom_call" | custom-call | tf_op jit(solution)/shard_map/write_out/pallas_call | solution.py:939

commit v3 on v2

--- a/solution.py
+++ b/solution.py
@@ -386,7 +386,7 @@
     g_v, m_v, f_v, s_v, x_v, n_v, w, acc, part, slots, sums, inv, kv, q_n, probs,
     far_x, far_inv, far_kv,
     load_sem, part_send, part_recv, sum_send, sum_recv, ready, p_send, q_send, y_send, c_send,
-    w_recv, far_send, far_recv,
+    z_recv, y_recv, c_recv, far_send, far_recv,
 ):
     me = lax.axis_index("dp")
     sec = lax.axis_index("pipe")
@@ -562,30 +562,71 @@
     root = np.float32(0.5) * np.sqrt(np.float32(count))
     clip = jnp.minimum(1.0, root / jnp.sqrt(square_sum + 1e-06))
 
-    def send(b, u, dst, sem):
-        h, c = u
-        here = w.at[h, pl.ds(pl.multiple_of(at(*b) * rows + c * chunk, chunk), chunk)]
-        return pltpu.make_async_remote_copy(
-            src_ref=here, dst_ref=here, send_sem=sem, recv_sem=w_recv.at[h, at(*b), c],
+    def span(b, u):
+        h, low, size = u
+        return w.at[h, pl.ds(pl.multiple_of(at(*b) * rows + low, chunk), size)]
+
+    def send(b, u, dst, sem, recv):
+        pltpu.make_async_remote_copy(
+            src_ref=span(b, u), dst_ref=span(b, u), send_sem=sem, recv_sem=recv,
             device_id={"dp": dst, "pipe": sec}, device_id_type=MESH,
-        )
-
+        ).start()
+
+    def wait(b, u, sem):
+        pltpu.make_async_copy(span(b, u), span(b, u), sem).wait()
+
+    def one(u):
+        return (u[0], u[1] * chunk, chunk)
+
+    low = turned * chunk
+    keys_of, values_of, turned_of = (0, 0, rows), (1, low, rows - low), (1, 0, low)
+    groups = [keys_of, values_of] + ([turned_of] if turned else [])
     beyond = jnp.where(z == 1, 2, 1)
 
-    def to_pair(b, u):
-        send(b, u, at(planes[1], line, core), p_send).start()
-
-    def to_beyond(b, u):
-        send(b, u, at(beyond, line, core), q_send).start()
-
-    def across(b, u):
-        send(b, u, at(z, 1 - line, core), y_send).start()
-
-    def beside(b, u):
-        send(b, u, at(z, line, 1 - core), c_send).start()
-
-    def arrived(b, u):
-        send(b, u, me, c_send).wait_recv()
+    def z_sem(s, u):
+        return z_recv.at[planes[s], u[0], u[1]]
+
+    def y_sem(s, g):
+        return y_recv.at[planes[s], groups.index(g)]
+
+    def to_pair(s, u):
+        send(here(s), one(u), at(planes[1], line, core), p_send, z_sem(s, u))
+
+    def to_beyond(s, u):
+        send(here(s), one(u), at(beyond, line, core), q_send, z_sem(s, u))
+
+    def turn_to_pair(s):
+        send(there(s), turned_of, at(planes[1], line, core), p_send, y_sem(s, turned_of))
+
+    def turn_to_beyond(s):
+        send(there(s), turned_of, at(beyond, line, core), q_send, y_sem(s, turned_of))
+
+    def across(s, u):
+        g = keys_of if u[0] == 0 else turned_of if u in turns else values_of
+        send(here(s), one(u), at(z, 1 - line, core), y_send, y_sem(s, g))
+
+    def beside(s, u):
+        send(here(s), one(u), at(z, line, 1 - core), c_send, c_recv.at[planes[s], u[0]])
+
+    def group_beside(s, g):
+        send(there(s), g, at(z, line, 1 - core), c_send, c_recv.at[planes[s], 2 + groups.index(g)])
+
+    def arrived(s, u):
+        wait(here(s), one(u), z_sem(s, u))
+
+    def group_arrived(s, g):
+        wait(there(s), g, y_sem(s, g))
+
+    def pass_groups(s, some):
+        for g in some:
+            group_arrived(s, g)
+            group_beside(s, g)
+
+    def side(s, h):
+        wait((planes[s], line, 1 - core), (h, 0, rows), c_recv.at[planes[s], h])
+
+    def side_group(s, g):
+        wait((planes[s], 1 - line, 1 - core), g, c_recv.at[planes[s], 2 + groups.index(g)])
 
     def here(s):
         return (planes[s], line, core)
@@ -611,19 +652,12 @@
         return jnp.dot(n_v[:, d], own, preferred_element_type=jnp.float32)
 
     def straight_values(s):
-        low = turned * chunk
         return product(1, s, 1 - line, 0, low, rows - low) + product(1, s, 1 - line, 1, low, rows - low)
 
     def multiply(s):
         acc[...] += product_line(s, line)
         acc[:, halves[0]] += product_line(s, 1 - line, 0)
         acc[:, halves[1]] += straight_values(s)
-
-    def from_beside(s, own_units, other_units):
-        for u in own_units:
-            arrived((planes[s], line, 1 - core), u)
-        for u in other_units:
-            arrived((planes[s], 1 - line, 1 - core), u)
 
     for h, c in units:
         r = pl.ds(c * chunk, chunk)
@@ -631,14 +665,14 @@
             0, r, slice(h * HEAD, (h + 1) * HEAD)
         ).astype(jnp.bfloat16)
         u = (h, c)
-        to_pair(here(0), u)
+        to_pair(0, u)
 
         @pl.when(inner)
         def _():
-            to_beyond(here(0), u)
-
-        across(here(0), u)
-        beside(here(0), u)
+            to_beyond(0, u)
+
+        across(0, u)
+        beside(0, u)
 
     head_copy.start()
     inv_copy.start()
@@ -650,69 +684,73 @@
                 update(b, pl.ds(c * chunk, chunk), slice(h * HEAD, (h + 1) * HEAD))
 
     for u in units:
-        arrived(here(1), u)
+        arrived(1, u)
 
         @pl.when(inner)
         def _():
-            to_beyond(here(1), u)
-            arrived(here(2), u)
-            to_pair(here(2), u)
-            beside(here(2), u)
+            to_beyond(1, u)
+            arrived(2, u)
+            to_pair(2, u)
+            beside(2, u)
 
         if u in straight:
-            across(here(1), u)
-        beside(here(1), u)
-        arrived(there(0), u)
-        beside(there(0), u)
+            across(1, u)
+        beside(1, u)
 
     @pl.when(inner)
     def _():
         for u in straight:
-            across(here(2), u)
-        for u in turns:
-            to_beyond(there(0), u)
-
-    @pl.when(outer)
-    def _():
-        for u in turns:
-            to_pair(there(0), u)
-
-    from_beside(0, units, units)
+            across(2, u)
+
+    pass_groups(0, groups)
+    if turned:
+
+        @pl.when(inner)
+        def _():
+            turn_to_beyond(0)
+
+        @pl.when(outer)
+        def _():
+            turn_to_pair(0)
+
+    for h in range(2):
+        side(0, h)
+    for g in groups:
+        side_group(0, g)
     acc[...] += product_line(0, line) + product_line(0, 1 - line)
 
     for u in units:
 
         @pl.when(inner)
         def _():
-            arrived(here(3), u)
-            to_pair(here(3), u)
-            across(here(3), u) if u in straight else None
-            beside(here(3), u)
+            arrived(3, u)
+            to_pair(3, u)
+            across(3, u) if u in straight else None
+            beside(3, u)
 
         @pl.when(outer)
         def _():
-            arrived(here(2), u)
-            across(here(2), u) if u in straight else None
-            beside(here(2), u)
-
-        if u in straight:
-            arrived(there(1), u)
-            beside(there(1), u)
-
-    @pl.when(inner)
-    def _():
-        for u in turns:
-            arrived(there(1), u)
-            to_beyond(there(1), u)
-            beside(there(1), u)
-            to_pair(there(0), u)
-        for s in (2, 3):
-            for u in turns:
-                arrived(there(s), u)
-                to_pair(there(s), u)
-                beside(there(s), u)
-
-    from_beside(1, units, straight)
+            arrived(2, u)
+            across(2, u) if u in straight else None
+            beside(2, u)
+
+    pass_groups(1, groups[:2])
+    if turned:
+
+        @pl.when(inner)
+        def _():
+            group_arrived(1, turned_of)
+            turn_to_beyond(1)
+            group_beside(1, turned_of)
+            turn_to_pair(0)
+            for s in (2, 3):
+                group_arrived(s, turned_of)
+                turn_to_pair(s)
+                group_beside(s, turned_of)
+
+    for h in range(2):
+        side(1, h)
+        side_group(1, groups[h])
     multiply(1)
     head_copy.wait_recv()
     inv_copy.wait_recv()
@@ -720,58 +758,44 @@
         hs = pl.ds(h * HEAD, HEAD)
         q_n[:, hs] = (far_x[:, hs].astype(jnp.float32) * far_inv[...]).astype(jnp.bfloat16)
 
-    for u in units:
+
+    @pl.when(outer)
+    def _():
+        for u in units:
+            arrived(3, u)
+            across(3, u) if u in straight else None
+            beside(3, u)
+
+    pass_groups(2, groups[:2])
+    for h in range(2):
+        side(2, h)
+        side_group(2, groups[h])
+    multiply(2)
+
+    side(3, 0)
+    acc[:, halves[0]] += product_line(3, line, 0)
+    pass_groups(3, [keys_of])
+    if turned:
 
         @pl.when(outer)
         def _():
-            arrived(here(3), u)
-            across(here(3), u) if u in straight else None
-            beside(here(3), u)
-
-        if u in straight:
-            arrived(there(2), u)
-            beside(there(2), u)
-
-    from_beside(2, units, straight)
-    multiply(2)
-
-    from_beside(3, [u for u in units if u[0] == 0], [])
-    acc[:, halves[0]] += product_line(3, line, 0)
-    for u in straight:
-        if u[0] == 0:
-            arrived(there(3), u)
-            beside(there(3), u)
-    from_beside(3, [], [u for u in units if u[0] == 0])
+            for s in (1, 2, 3):
+                pass_groups(s, [turned_of])
+
+    side_group(3, keys_of)
     kv[0] = (acc[:, halves[0]] + product_line(3, 1 - line, 0)).astype(jnp.bfloat16)
     k_copy = to_next(kv.at[0], far_kv.at[0], 2)
     k_copy.start()
-    from_beside(3, [u for u in units if u[0] == 1], [])
+    side(3, 1)
     acc[:, halves[1]] += product_line(3, line, 1)
-    last = [u for u in straight if u[0] == 1]
-
-    def turns_here():
-        @pl.when(outer)
-        def _():
-            for s in (1, 2, 3):
-                for u in turns:
-                    arrived(there(s), u)
-                    beside(there(s), u)
-
-    for u in last[:-1]:
-        arrived(there(3), u)
-        beside(there(3), u)
-    turns_here()
-    arrived(there(3), last[-1])
-    beside(there(3), last[-1])
+    pass_groups(3, [values_of])
     if turned:
         for s in (1, 2, 3):
-            for u in turns:
-                arrived((planes[s], 1 - line, 1 - core), u)
+            side_group(s, turned_of)
         acc[:, halves[1]] += sum(
-            product(1, s, 1 - line, cc, 0, turned * chunk) for s in (1, 2, 3) for cc in range(cores)
+            product(1, s, 1 - line, cc, 0, low) for s in (1, 2, 3) for cc in range(cores)
         )
-    for u in last:
-        arrived((planes[3], 1 - line, 1 - core), u)
+    side_group(3, values_of)
     kv[1] = (acc[:, halves[1]] + straight_values(3)).astype(jnp.bfloat16)
     v_copy = to_next(kv.at[1], far_kv.at[1], 3)
     v_copy.start()
@@ -813,8 +837,8 @@
             lift(zz).wait_send()
 
     def sent(n, sem):
-        span = w.at[0, pl.ds(0, n * chunk)]
-        pltpu.make_async_copy(span, span, sem).wait()
+        whole = w.at[0, pl.ds(0, n * chunk)]
+        pltpu.make_async_copy(whole, whole, sem).wait()
 
     n, t = len(units), len(turns)
 
@@ -891,7 +915,9 @@
             dma,
             dma,
             dma,
-            dma((2, n_dp, rows // CHUNK)),
+            dma((depth, 2, rows // CHUNK)),
+            dma((depth, 3)),
+            dma((depth, 5)),
             dma((4,)),
             dma((4,)),
         ]

time: 41.5 us -> 40.8 us (0.983)
  Pallas kernels: 40.7 us -> 40 us
    pallas_call x1, Pallas kernels: 38.9 us -> 38.2 us  [on_device(): pl.pallas_call(body, out_shape=tuple((pltpu.VMEM(v.shape, v.dtype) for v...]
where the time goes in v3:
time: 40.8 us; the launch traced here: 40.6 us
  Pallas kernels  40 us (98%)
  between operations  0.64 us (2%)
    pallas_call x1, Pallas kernels, on_device(): pl.pallas_call(body, out_shape=tuple((pltpu.VMEM(v.shape, v.dtype) for v...  38.2 us
    pallas_call x1, Pallas kernels, on_device(): pl.pallas_call(write_out, out_shape=shapes, in_specs=[vmem] * 4, out_spec...  1.8 us

profile of v3, /device:TPU:0, one launch (start us, length us, event | category | flops | bytes accessed | tf_op | source)
XLA Modules:
  0.0 40.6 jit_solution(4059834832881220370)
XLA Ops:
  0.6 38.2 %section.1 = (f32[1,2,512,256]{3,2,1,0:T(8,128)S(1)}, f32[1,2,512,256]{3,2,1,0:T(8,128)S(1)}, f32[1,2,512,256]{3,2,1,0:T(8,128)S(1)}, bf16[1,168,1024]{2,1,0:T(8,128)(2,1)S(1)}) custom-call(f32[1,2,512,256]{3,2,1,0:T(8,128)} %master.1, f32[1,2,512,256]{3,2,1,0:T(8,128)} %grads.1, f32[1,2,512,256]{3,2,1,0:T(8,128)} %first.1, f32[1,2,512,256]{3,2,1,0:T(8,128)} %second.1, ...), custom_call_target="tpu_custom_call" | custom-call | tf_op jit(solution)/shard_map/section/pallas_call | solution.py:954
  38.8 1.8 %write_out.1 = (f32[1,2,512,256]{3,2,1,0:T(8,128)}, f32[1,2,512,256]{3,2,1,0:T(8,128)}, f32[1,2,512,256]{3,2,1,0:T(8,128)}, bf16[1,168,1024]{2,1,0:T(8,128)(2,1)}) custom-call(f32[1,2,512,256]{3,2,1,0:T(8,128)S(1)} %get-tuple-element.8.refs_0_, f32[1,2,512,256]{3,2,1,0:T(8,128)S(1)} %get-tuple-element.9.refs_1_, ...), custom_call_target="tpu_custom_call" | custom-call | tf_op jit(solution)/shard_map/write_out/pallas_call | solution.py:965
